TPU v7x, 256 devices: a whole 4x4x8 slice. The times are simulated.
256 devices in a mesh: ep: 64 (over z, y, core), rep: 4 (over x).
Axes of the slice: x: 4, y: 4, z: 8, core: 2. Of those that a mesh axis runs over, the one named last changes fastest.
Arguments:
- residual: bfloat16 [4096, 2048], P('ep'), may hold values from -6 to 6
- query_latent: bfloat16 [4096, 8192], P(('ep', 'rep')), may hold values from -32.5 to 32.5
- query_rope: bfloat16 [4096, 1024], P(('ep', 'rep')), may hold values from -4 to 4
- cache_latent: bfloat16 [8192, 32, 512], P(('ep', 'rep')), may hold values from -4.6 to 4.6
- cache_rope: bfloat16 [8192, 2048], P(('ep', 'rep')), may hold values from -4 to 4
- page_table: int32 [4096, 9], P(('ep', 'rep')), may hold values from 0 to 31, as said below
- lengths: int32 [4096], P(('ep', 'rep')), may hold values from 257 to 288, as said below
- value_up: bfloat16 [16, 512, 128], P('rep'), may hold values from -0.25 to 0.25
- out_proj: bfloat16 [2048, 2048], P('rep'), may hold values from -0.125 to 0.125
- routes: int32 [4096, 6], P('ep'), may hold values from 0 to 63, all different within a row; in each aligned block of 64 rows (0 to 63, 64 to 127, ...) at most 12 rows name the same one
- route_weight: float32 [4096, 6], P('ep'), may hold values from 0.05 to 0.6
- placement: int32 [64], replicated, may hold values from 0 to 63, each once
- expert_gate: bfloat16 [64, 2048, 1408], P('ep', None, 'rep'), may hold values from -0.125 to 0.125
- expert_up: bfloat16 [64, 2048, 1408], P('ep', None, 'rep'), may hold values from -0.125 to 0.125
- expert_down: bfloat16 [64, 1408, 2048], P('ep', 'rep'), may hold values from -0.15625 to 0.15625
- shared_gate: bfloat16 [2048, 1408], P(None, 'rep'), may hold values from -0.125 to 0.125
- shared_up: bfloat16 [2048, 1408], P(None, 'rep'), may hold values from -0.125 to 0.125
- shared_down: bfloat16 [1408, 2048], P('rep'), may hold values from -0.15625 to 0.15625
- norm_gain: float32 [2048], replicated, may hold values from 0.5 to 1.5
Outputs:
- normed: bfloat16 [4096, 2048], P(('ep', 'rep'))
Inputs may be any that keep to these rules, and one draw needn't show every extreme that they name: `page_table`: entries number the 32 pages of the row's own device. A device's rows come in consecutive groups of 8 that share their first 8 entries; all other entries of a device are distinct. `lengths`: every row's context covers its shared prompt; the last row of every device has the greatest length. `routes`: within the 64 rows of one index of ep, no expert is named by more than 12 rows, a bound that some block reaches. `placement`: each slot holds exactly one expert.
All inputs are finite; a program needn't handle non-finite values.
Results may differ from a plain program's by a relative error of at most 0.014.
Values may be sent and summed in bfloat16 or wider, within the bound.
A program may use at most 128 MiB of HBM per device.

v0:
```python
import math
import jax
import jax.numpy as jnp
from jax import lax
from jax.sharding import PartitionSpec as P

ROPE = 64
VHEAD = 128
EPSILON = 1e-06


def attend_rows(query_latent, query_rope, cache_latent, cache_rope, page_table, lengths):
    row_count = page_table.shape[0]
    page_len = cache_latent.shape[1]
    latent_width = cache_latent.shape[2]
    rope_width = cache_rope.shape[1] // page_len
    head_count = query_rope.shape[1] // rope_width
    key_span = page_table.shape[1] * page_len
    keys_lat = cache_latent[page_table].reshape(row_count, key_span, latent_width)
    keys_rope = cache_rope[page_table].reshape(row_count, key_span, rope_width)
    query_lat = query_latent.reshape(row_count, head_count, latent_width)
    query_rot = query_rope.reshape(row_count, head_count, rope_width)
    score_scale = 1.0 / math.sqrt(VHEAD + ROPE)
    scores = (
        jnp.einsum("thr,tlr->thl", query_lat, keys_lat, preferred_element_type=jnp.float32)
        + jnp.einsum("thr,tlr->thl", query_rot, keys_rope, preferred_element_type=jnp.float32)
    ) * score_scale
    live_mask = (jnp.arange(key_span, dtype=jnp.int32)[None, :] < lengths[:, None])[:, None, :]
    masked = jnp.where(live_mask, scores, -jnp.inf)
    row_peak = jnp.max(masked, axis=2, keepdims=True)
    expons = jnp.where(live_mask, jnp.exp(scores - row_peak), 0.0)
    probs = (expons / jnp.sum(expons, axis=2, keepdims=True)).astype(jnp.bfloat16)
    latent_out = jnp.einsum("thl,tlr->thr", probs, keys_lat, preferred_element_type=jnp.float32)
    return latent_out.astype(jnp.bfloat16)


def per_device(
    residual,
    query_latent,
    query_rope,
    cache_latent,
    cache_rope,
    page_table,
    lengths,
    value_up,
    out_proj,
    routes,
    route_weight,
    placement,
    expert_gate,
    expert_up,
    expert_down,
    shared_gate,
    shared_up,
    shared_down,
    norm_gain,
):
    replicas = lax.axis_size("rep")
    expert_groups = lax.axis_size("ep")
    latent_out = attend_rows(
        query_latent, query_rope, cache_latent, cache_rope, page_table, lengths
    )
    own_count = latent_out.shape[0]
    swapped = lax.all_to_all(latent_out, "rep", split_axis=1, concat_axis=0, tiled=True)
    group_rows = swapped.shape[0]
    head_out = jnp.einsum(
        "thr,hrv->thv", swapped, value_up, preferred_element_type=jnp.float32
    ).astype(jnp.bfloat16)
    attn_terms = jnp.dot(
        head_out.reshape(group_rows, -1), out_proj, preferred_element_type=jnp.float32
    )
    attended = lax.psum(attn_terms.astype(jnp.bfloat16), "rep")
    hidden = (residual.astype(jnp.float32) + attended.astype(jnp.float32)).astype(jnp.bfloat16)
    model_width = hidden.shape[1]
    shared_act = (
        jax.nn.silu(jnp.dot(hidden, shared_gate, preferred_element_type=jnp.float32))
        * jnp.dot(hidden, shared_up, preferred_element_type=jnp.float32)
    ).astype(jnp.bfloat16)
    shared_terms = jnp.dot(shared_act, shared_down, preferred_element_type=jnp.float32)
    experts = placement.shape[0]
    route_count = routes.shape[1]
    per_group = experts // expert_groups
    capacity = max(
        replicas, min(group_rows, 2 * group_rows * route_count // experts // replicas * replicas)
    )
    expert_ids = jnp.arange(experts, dtype=jnp.int32)
    slot_index = jnp.sum(jnp.where(routes[:, :, None] == expert_ids, placement, 0), axis=2).reshape(
        -1
    )
    one_hot = (slot_index[:, None] == expert_ids[None, :]).astype(jnp.int32)
    earlier = jnp.cumsum(one_hot, axis=0) - one_hot
    position = jnp.sum(earlier * one_hot, axis=1)
    assignments = slot_index.shape[0]
    source_row = (
        jnp.full((experts * capacity,), group_rows, jnp.int32)
        .at[slot_index * capacity + position]
        .set(jnp.arange(assignments, dtype=jnp.int32) // route_count)
    )
    padded = jnp.concatenate([hidden, jnp.zeros((1, model_width), jnp.bfloat16)], axis=0)
    outgoing = padded[source_row].reshape(expert_groups, per_group * capacity, model_width)
    incoming = lax.all_to_all(outgoing, "ep", split_axis=0, concat_axis=0, tiled=True).reshape(
        expert_groups, per_group, capacity, model_width
    )
    gate_values = jnp.einsum(
        "secd,edf->secf", incoming, expert_gate, preferred_element_type=jnp.float32
    )
    up_values = jnp.einsum(
        "secd,edf->secf", incoming, expert_up, preferred_element_type=jnp.float32
    )
    activated = (jax.nn.silu(gate_values) * up_values).astype(jnp.bfloat16)
    expert_terms = jnp.einsum(
        "secf,efd->secd", activated, expert_down, preferred_element_type=jnp.float32
    )
    outbound = expert_terms.astype(jnp.bfloat16).reshape(
        expert_groups, per_group * capacity, model_width
    )
    returned = lax.all_to_all(outbound, "ep", split_axis=0, concat_axis=0, tiled=True)
    picked = returned.reshape(experts * capacity, model_width)[slot_index * capacity + position]
    weight_used = route_weight.reshape(-1)
    routed = jnp.sum(
        (picked.astype(jnp.float32) * weight_used[:, None]).reshape(
            group_rows, route_count, model_width
        ),
        axis=1,
    )
    row_sums = lax.psum_scatter(
        (routed + shared_terms).astype(jnp.bfloat16), "rep", scatter_dimension=0, tiled=True
    ).astype(jnp.float32)
    own_hidden = lax.dynamic_slice_in_dim(hidden, lax.axis_index("rep") * own_count, own_count, 0)
    mixed = row_sums + own_hidden.astype(jnp.float32)
    inverse = lax.rsqrt(jnp.mean(mixed * mixed, axis=1, keepdims=True) + EPSILON)
    return (mixed * inverse * norm_gain).astype(jnp.bfloat16)


def solution(mesh):
    in_specs = (
        P("ep", None),
        P(("ep", "rep"), None),
        P(("ep", "rep"), None),
        P(("ep", "rep"), None, None),
        P(("ep", "rep"), None),
        P(("ep", "rep"), None),
        P(("ep", "rep")),
        P("rep", None, None),
        P("rep", None),
        P("ep", None),
        P("ep", None),
        P(),
        P("ep", None, "rep"),
        P("ep", None, "rep"),
        P("ep", "rep", None),
        P(None, "rep"),
        P(None, "rep"),
        P("rep", None),
        P(),
    )
    out_specs = P(("ep", "rep"), None)
    return jax.shard_map(
        per_device, mesh=mesh, in_specs=in_specs, out_specs=out_specs, check_vma=False
    )
```

profile of v0, /device:TPU:8, one launch (start us, length us, event | category | flops | bytes accessed | tf_op | source)
XLA Modules:
  0.0 386.6 jit_solution(4769839513103228752)
XLA Ops:
  6.5 0.0 copy-start
  6.5 0.8 compare_select_fusion
  7.4 0.1 reshape.143
  7.5 1.0 copy.57
  8.5 0.0 copy-start.1
  8.5 8.8 %gather_fusion = bf16[144,32,512]{2,1,0:T(8,128)(2,1)} fusion(bf16[32,32,512]{2,1,0:T(8,128)(2,1)} %param.22, s32[1024]{0:T(1024)S(1)} %pad_clamp_fusion.2), kind=kCustom, calls=%fused_computation | custom fusion | bytes 9437760 | tf_op jit(solution)/shard_map/gather | solution.py:19
  17.3 0.0 copy-done.1
  17.3 1.8 gather_fusion.1
  19.2 2.2 reshape.130
  21.4 1.5 reshape.131
  22.9 0.0 copy-done.11
  22.9 0.1 iota_compare_fusion.3
  23.0 3.7 fusion.79
  26.7 0.0 copy-done.6
  26.7 0.5 fusion.36
  27.1 0.0 copy-start.3
  27.1 0.8 copy-done.3
  27.9 0.2 fusion.78
  28.1 0.0 copy-start.9
  28.1 0.0 copy-start.10
  28.2 3.5 convolution_convert_fusion.2
  31.7 0.9 copy.43
  32.6 4.3 %all-to-all-start = ((bf16[16,16,512]{2,0,1:T(8,128)(2,1)}), bf16[16,16,512]{2,0,1:T(8,128)(2,1)S(1)}, u32[]{:S(2)}, u32[]{:S(2)}) async-start(bf16[16,16,512]{2,0,1:T(8,128)(2,1)} %copy.43), calls=%async_computation | async-start | bytes 524288 | tf_op jit(solution)/shard_map/all_to_all | solution.py:64
  36.9 0.3 select_reduce_fusion.1
  37.1 0.1 copy.47
  37.2 0.1 eq.45
  37.4 0.1 eq.41
  37.6 0.9 reduce-window.6
  38.5 0.2 slice_reduce_fusion
  38.7 0.1 copy.46
  38.8 0.1 mul.72
  39.0 0.1 fusion.52
  39.1 2.9 scatter_custom_fusion
  42.1 1.5 all-to-all-done
  43.6 0.0 copy-start.5
  43.6 0.2 fusion.40
  43.8 0.0 copy-done
  43.8 1.2 convolution_convert_fusion.1
  45.0 0.0 all-reduce.3.cloned.1.call-update
  45.1 48.8 %all-reduce.3.cloned.1.call-done = bf16[64,2048]{1,0:T(8,128)(2,1)} async-done(((bf16[64,2048]{1,0:T(8,128)(2,1)}), bf16[64,2048]{1,0:T(8,128)(2,1)}) %all-reduce.3.cloned.1.call-update) | async-done | bytes 262160 | tf_op jit(solution)/shard_map/psum | solution.py:72
  93.9 1.0 add_convert_fusion
  94.9 4.3 %gather_fusion.2 = bf16[768,2048]{1,0:T(8,128)(2,1)} fusion(bf16[65,2048]{1,0:T(8,128)(2,1)S(1)} %concatenate.3, s32[1024]{0:T(1024)S(1)} %pad_clamp_fusion.1), kind=kCustom, calls=%fused_computation.2 | custom fusion | bytes 6294528 | tf_op jit(solution)/shard_map/gather | solution.py:100
  99.2 6.1 %reshape.134 = bf16[64,12,2048]{2,1,0:T(8,128)(2,1)} reshape(bf16[768,2048]{1,0:T(8,128)(2,1)} %gather_fusion.2) | data formatting | bytes 6291456 | tf_op jit(solution)/shard_map/reshape | solution.py:100
  105.3 106.9 %all_to_all.28 = bf16[64,12,2048]{2,1,0:T(8,128)(2,1)S(1)} all-to-all(bf16[64,12,2048]{2,1,0:T(8,128)(2,1)} %reshape.134), channel_id=1, replica_groups=mesh['ep'=64,'rep'=4] {'ep'}, dimensions={0} | all-to-all | bytes 6291456 | tf_op jit(solution)/shard_map/all_to_all | solution.py:101
  212.1 2.0 copy-done.2
  214.2 3.1 fusion.9
  217.2 8.8 %convolution_convert_fusion = bf16[64,12,2048]{2,0,1:T(8,128)(2,1)} fusion(bf16[1,352,2048]{2,1,0:T(8,128)(2,1)} %param.33, bf16[1,2048,352]{1,2,0:T(8,128)(2,1)} %param.32, bf16[64,12,2048]{2,1,0:T(8,128)(2,1)} %copy-done.2, f32[64,1,12,352]{3,0,2,1:T(8,128)} %fusion.9), kind=kOutput, calls=%fused_computation.7 | convolution fusion | flops 2217787392 | bytes 10256384 | tf_op jit(solution)/shard_map/secf,efd->secd/dot_general | solution.py:111
  226.0 5.7 %copy.52 = bf16[64,12,2048]{2,1,0:T(8,128)(2,1)} copy(bf16[64,12,2048]{2,0,1:T(8,128)(2,1)} %convolution_convert_fusion) | data formatting | bytes 6291456 | tf_op jit(solution)/shard_map/convert_element_type | solution.py:114
  231.7 5.8 %all-to-all-start.2 = ((bf16[64,12,2048]{2,1,0:T(8,128)(2,1)}), bf16[64,12,2048]{2,1,0:T(8,128)(2,1)}, u32[]{:S(2)}, u32[]{:S(2)}) async-start(bf16[64,12,2048]{2,1,0:T(8,128)(2,1)} %copy.52), calls=%async_computation.2 | async-start | bytes 8388608 | tf_op jit(solution)/shard_map/all_to_all | solution.py:117
  237.4 0.3 reduce-scatter.2.cloned.1.call-start
  237.7 0.1 copy.53
  237.8 1.9 fusion.80
  239.7 93.9 %all-to-all-done.2 = bf16[64,12,2048]{2,1,0:T(8,128)(2,1)} async-done(((bf16[64,12,2048]{2,1,0:T(8,128)(2,1)}), bf16[64,12,2048]{2,1,0:T(8,128)(2,1)}, u32[]{:S(2)}, u32[]{:S(2)}) %all-to-all-start.2) | async-done | bytes 3145760 | tf_op jit(solution)/shard_map/all_to_all | solution.py:117
  333.6 6.2 %reshape.139 = bf16[768,2048]{1,0:T(8,128)(2,1)} reshape(bf16[64,12,2048]{2,1,0:T(8,128)(2,1)} %all-to-all-done.2) | data formatting | bytes 6291456 | tf_op jit(solution)/shard_map/reshape | solution.py:118
  339.8 7.4 %gather_fusion.3 = bf16[384,2048]{1,0:T(8,128)(2,1)} fusion(bf16[768,2048]{1,0:T(8,128)(2,1)} %reshape.139, s32[1024]{0:T(1024)S(1)} %pad_clamp_fusion), kind=kCustom, calls=%fused_computation.3 | custom fusion | bytes 3147264 | tf_op jit(solution)/shard_map/gather | solution.py:118
  347.1 3.9 %reshape.140 = f32[64,6,2048]{2,1,0:T(8,128)} reshape(bf16[384,2048]{1,0:T(8,128)(2,1)} %gather_fusion.3) | data formatting | bytes 4718592 | tf_op jit(solution)/shard_map/convert_element_type | solution.py:121
  351.1 3.7 multiply_reduce_fusion
  354.8 0.0 copy-start.7
  354.8 3.7 fusion.1
  358.5 0.0 reduce-scatter.2.cloned.1.call-update
  358.5 18.6 %reduce-scatter.2.cloned.1.call-done = bf16[16,2048]{1,0:T(8,128)(2,1)} async-done(((bf16[64,2048]{1,0:T(8,128)(2,1)}), bf16[16,2048]{1,0:T(8,128)(2,1)}) %reduce-scatter.2.cloned.1.call-update) | async-done | bytes 65552 | tf_op jit(solution)/shard_map/reduce_scatter | solution.py:126
  377.2 1.0 multiply_reduce_fusion.1
  378.1 0.0 copy-done.7
  378.2 1.6 multiply_convert_fusion
  (25 shorter events, 0.2 us)
Async XLA Ops:
  6.5 37.3 %copy-start = (bf16[512,2048]{1,0:T(8,128)(2,1)S(1)}, bf16[512,2048]{1,0:T(8,128)(2,1)}, u32[]{:S(2)}) copy-start(bf16[512,2048]{1,0:T(8,128)(2,1)} %param.27) | copy-start | bytes 6291460
  8.5 8.8 %copy-start.1 = (bf16[32,2048]{1,0:T(8,128)(2,1)S(1)}, bf16[32,2048]{1,0:T(8,128)(2,1)}, u32[]{:S(2)}) copy-start(bf16[32,2048]{1,0:T(8,128)(2,1)} %param.23) | copy-start | bytes 393220
  19.2 3.7 copy-start.11
  23.0 3.7 copy-start.6
  27.1 0.8 copy-start.3
  28.1 8.7 %copy-start.9 = (s32[64,6]{0,1:T(8,128)S(1)}, s32[64,6]{0,1:T(8,128)}, u32[]{:S(2)}) copy-start(s32[64,6]{0,1:T(8,128)} %param.28) | copy-start | bytes 4612
  28.1 8.7 %copy-start.10 = (s32[64]{0:T(128)S(1)}, s32[64]{0:T(128)}, u32[]{:S(2)}) copy-start(s32[64]{0:T(128)} %param.30) | copy-start | bytes 772
  31.7 11.9 %copy-start.4 = (bf16[4,512,128]{2,1,0:T(8,128)(2,1)S(1)}, bf16[4,512,128]{2,1,0:T(8,128)(2,1)}, u32[]{:S(2)}) copy-start(bf16[4,512,128]{2,1,0:T(8,128)(2,1)} %param.26) | copy-start | bytes 1572868
  32.6 11.0 %all-to-all-start = ((bf16[16,16,512]{2,0,1:T(8,128)(2,1)}), bf16[16,16,512]{2,0,1:T(8,128)(2,1)S(1)}, u32[]{:S(2)}, u32[]{:S(2)}) async-start(bf16[16,16,512]{2,0,1:T(8,128)(2,1)} %copy.43), calls=%async_computation | async-start | bytes 524288 | tf_op jit(solution)/shard_map/all_to_all | solution.py:64
  36.9 57.0 %all-reduce.3.cloned.1.call-start = ((), (), s32[]{:S(2)}) async-start(), calls=%async_computation.4 | async-start | bytes 524288 | tf_op jit(solution)/shard_map/psum | solution.py:72
  43.6 50.3 %copy-start.5 = (bf16[64,2048]{1,0:T(8,128)(2,1)S(1)}, bf16[64,2048]{1,0:T(8,128)(2,1)}, u32[]{:S(2)}) copy-start(bf16[64,2048]{1,0:T(8,128)(2,1)} %param.19) | copy-start | bytes 786436
  105.3 108.9 %copy-start.12 = (bf16[1,2048,352]{1,2,0:T(8,128)(2,1)S(1)}, bf16[1,2048,352]{1,2,0:T(8,128)(2,1)}, u32[]{:S(2)}) copy-start(bf16[1,2048,352]{1,2,0:T(8,128)(2,1)} %param.31) | copy-start | bytes 4325380
  212.1 2.0 copy-start.2
  231.7 6.0 %copy-start.8 = (f32[64,6]{0,1:T(8,128)S(1)}, f32[64,6]{0,1:T(8,128)}, u32[]{:S(2)}) copy-start(f32[64,6]{0,1:T(8,128)} %param.29) | copy-start | bytes 4612
  231.7 101.9 %all-to-all-start.2 = ((bf16[64,12,2048]{2,1,0:T(8,128)(2,1)}), bf16[64,12,2048]{2,1,0:T(8,128)(2,1)}, u32[]{:S(2)}, u32[]{:S(2)}) async-start(bf16[64,12,2048]{2,1,0:T(8,128)(2,1)} %copy.52), calls=%async_computation.2 | async-start | bytes 8388608 | tf_op jit(solution)/shard_map/all_to_all | solution.py:117
  237.4 139.7 %reduce-scatter.2.cloned.1.call-start = ((), (), s32[]{:S(2)}) async-start(), calls=%async_computation.5 | async-start | bytes 327680 | tf_op jit(solution)/shard_map/reduce_scatter | solution.py:126
  354.8 23.3 %copy-start.7 = (f32[2048]{0:T(1024)S(1)}, f32[2048]{0:T(1024)}, u32[]{:S(2)}) copy-start(f32[2048]{0:T(1024)} %param.37) | copy-start | bytes 24580
Sparse Core Ops, SparseCore 0:
  45.2 48.6 all-reduce.2
  358.6 18.4 reduce-scatter.1
where the time goes:
time: 388 us; the launch traced here: 387 us
  waiting for transfers between devices  163 us (42%)
  blocking collectives  107 us (28%)
  local copies, waits for them, and re-layouts  56.5 us (15%)
  matrix products  26.6 us (7%)
  between operations  13.7 us (4%)
  starting transfers between devices  10.3 us (3%)
  other arithmetic  9.84 us (3%)
    all_to_all x1, blocking collectives, per_device(): lax.all_to_all(outgoing, 'ep', split_axis=0, concat_axis=0, tiled=True)  107 us
    all_to_all x1, waiting for transfers between devices, per_device(): lax.all_to_all(outbound, 'ep', split_axis=0, concat_axis=0, tiled=True)  93.9 us
    psum x1, waiting for transfers between devices, per_device(): attended = lax.psum(attn_terms.astype(jnp.bfloat16), 'rep')  48.8 us
    reduce_scatter x1, waiting for transfers between devices, per_device(): lax.psum_scatter((routed + shared_terms).astype(jnp.bfloat16), 'rep', sca...  18.6 us
    dot_general x1, matrix products, per_device(): jnp.einsum('secf,efd->secd', activated, expert_down, preferred_element_ty...  8.8 us
    gather x1, local copies, waits for them, and re-layouts, attend_rows(): cache_latent[page_table].reshape(row_count, key_span, latent_width)  8.79 us
  transfers between devices with their start and end apart: 4, of which 4 were waited for; matrix products, arithmetic and copies ran while one was open for 2% of the time, Pallas kernels for 0%

commit v1 on v0

--- a/solution.py
+++ b/solution.py
@@ -69,7 +69,8 @@
     attn_terms = jnp.dot(
         head_out.reshape(group_rows, -1), out_proj, preferred_element_type=jnp.float32
     )
-    attended = lax.psum(attn_terms.astype(jnp.bfloat16), "rep")
+    obj = attn_terms.astype(jnp.bfloat16)
+    attended = jnp.sum(lax.all_gather(obj, "rep"), 0)
     hidden = (residual.astype(jnp.float32) + attended.astype(jnp.float32)).astype(jnp.bfloat16)
     model_width = hidden.shape[1]
     shared_act = (

time: 388 us -> 366 us (0.943)
  waiting for transfers between devices: 163 us -> 135 us
  blocking collectives: 107 us -> 118 us
  starting transfers between devices: 10.3 us -> 6.02 us
    psum x1 -> x0, waiting for transfers between devices: 48.8 us -> none  [per_device(): attended = lax.psum(attn_terms.astype(jnp.bfloat16), 'rep')]
    all_gather x0 -> x1, waiting for transfers between devices: none -> 22.4 us  [per_device(): attended = jnp.sum(lax.all_gather(obj, 'rep'), 0)]
    all_to_all x0 -> x1, blocking collectives: none -> 10.8 us  [per_device(): lax.all_to_all(latent_out, 'rep', split_axis=1, concat_axis=0, tiled=True)]
    all_to_all x1 -> x0, starting transfers between devices: 4.29 us -> none  [per_device(): lax.all_to_all(latent_out, 'rep', split_axis=1, concat_axis=0, tiled=True)]
  transfers between devices with their start and end apart: 4 -> 3, of which waited for: 4 -> 3; matrix products, arithmetic and copies ran while one was open for 2% -> 2% of each run, Pallas kernels for 0% -> 0%
where the time goes in v1:
time: 366 us; the launch traced here: 365 us
  waiting for transfers between devices  135 us (37%)
  blocking collectives  118 us (32%)
  local copies, waits for them, and re-layouts  55.8 us (15%)
  matrix products  26.6 us (7%)
  between operations  13.7 us (4%)
  other arithmetic  10.3 us (3%)
  starting transfers between devices  6.02 us (2%)
    all_to_all x1, blocking collectives, per_device(): lax.all_to_all(outgoing, 'ep', split_axis=0, concat_axis=0, tiled=True)  107 us
    all_to_all x1, waiting for transfers between devices, per_device(): lax.all_to_all(outbound, 'ep', split_axis=0, concat_axis=0, tiled=True)  93.9 us
    all_gather x1, waiting for transfers between devices, per_device(): attended = jnp.sum(lax.all_gather(obj, 'rep'), 0)  22.4 us
    reduce_scatter x1, waiting for transfers between devices, per_device(): lax.psum_scatter((routed + shared_terms).astype(jnp.bfloat16), 'rep', sca...  18.5 us
    all_to_all x1, blocking collectives, per_device(): lax.all_to_all(latent_out, 'rep', split_axis=1, concat_axis=0, tiled=True)  10.8 us
    dot_general x1, matrix products, per_device(): jnp.einsum('secf,efd->secd', activated, expert_down, preferred_element_ty...  8.8 us
    gather x1, local copies, waits for them, and re-layouts, attend_rows(): cache_latent[page_table].reshape(row_count, key_span, latent_width)  8.79 us
    gather x1, local copies, waits for them, and re-layouts, per_device(): returned.reshape(experts * capacity, model_width)  7.37 us
  transfers between devices with their start and end apart: 3, of which 3 were waited for; matrix products, arithmetic and copies ran while one was open for 2% of the time, Pallas kernels for 0%

profile of v1, /device:TPU:8, one launch (start us, length us, event | category | flops | bytes accessed | tf_op | source)
XLA Modules:
  0.0 364.8 jit_solution(3243508446039053008)
XLA Ops:
  6.5 0.0 copy-start
  6.5 0.0 all-gather.3.cloned.1.call-start
  6.5 0.8 compare_select_fusion
  7.4 0.1 reshape.143
  7.5 1.0 copy.57
  8.5 0.0 copy-start.1
  8.5 8.8 %gather_fusion = bf16[144,32,512]{2,1,0:T(8,128)(2,1)} fusion(bf16[32,32,512]{2,1,0:T(8,128)(2,1)} %param.22, s32[1024]{0:T(1024)S(1)} %pad_clamp_fusion.2), kind=kCustom, calls=%fused_computation | custom fusion | bytes 9437760 | tf_op jit(solution)/shard_map/gather | solution.py:19
  17.3 0.0 copy-done.1
  17.3 1.8 gather_fusion.1
  19.2 2.2 reshape.130
  21.4 1.5 reshape.131
  22.9 0.1 iota_compare_fusion.3
  23.0 3.7 %fusion.79 = f32[16,288,16]{1,2,0:T(8,128)S(1)} fusion(bf16[16,288,512]{2,1,0:T(8,128)(2,1)} %bitcast.101, bf16[16,16,512]{2,1,0:T(8,128)(2,1)S(1)} %bitcast.106), kind=kOutput, calls=%fused_computation.89 | convolution fusion | flops 75497472 | bytes 5275648 | tf_op jit(solution)/shard_map/thr,tlr->thl/dot_general | solution.py:25
  26.7 0.5 fusion.36
  27.1 0.0 copy-start.3
  27.1 0.8 copy-done.3
  27.9 0.2 fusion.78
  28.1 3.5 convolution_convert_fusion.2
  31.7 0.2 copy.43
  31.9 10.8 %all_to_all.28 = bf16[16,16,512]{2,0,1:T(8,128)(2,1)S(1)} all-to-all(bf16[16,16,512]{2,0,1:T(8,128)(2,1)S(1)} %copy.43), channel_id=1, replica_groups=mesh['ep'=64,'rep'=4] {'rep'}, dimensions={1} | all-to-all | bytes 524288 | tf_op jit(solution)/shard_map/all_to_all | solution.py:64
  42.7 0.0 copy-start.9
  42.7 0.0 copy-start.10
  42.7 0.2 fusion.40
  42.9 0.0 copy-done
  42.9 1.2 convolution_convert_fusion.1
  44.1 0.0 all-gather.3.cloned.1.call-update
  44.2 0.3 select_reduce_fusion.1
  44.4 0.1 copy.47
  44.5 0.1 eq.45
  44.7 0.1 eq.41
  44.8 0.9 reduce-window.6
  45.7 0.2 slice_reduce_fusion
  46.0 0.1 copy.46
  46.1 0.1 mul.72
  46.3 0.1 fusion.52
  46.4 2.9 scatter_custom_fusion
  49.4 22.4 %all-gather.3.cloned.1.call-done = bf16[256,2048]{1,0:T(8,128)(2,1)} async-done(((bf16[64,2048]{1,0:T(8,128)(2,1)}), bf16[256,2048]{1,0:T(8,128)(2,1)}) %all-gather.3.cloned.1.call-update) | async-done | bytes 1048592 | tf_op jit(solution)/shard_map/all_gather | solution.py:73
  71.8 1.4 reduce_sum.60
  73.2 0.0 copy-done.5
  73.2 0.1 add_convert_fusion
  73.3 4.3 %gather_fusion.2 = bf16[768,2048]{1,0:T(8,128)(2,1)} fusion(bf16[65,2048]{1,0:T(8,128)(2,1)S(1)} %concatenate.3, s32[1024]{0:T(1024)S(1)} %pad_clamp_fusion.1), kind=kCustom, calls=%fused_computation.2 | custom fusion | bytes 6294528 | tf_op jit(solution)/shard_map/gather | solution.py:101
  77.6 6.1 %reshape.134 = bf16[64,12,2048]{2,1,0:T(8,128)(2,1)} reshape(bf16[768,2048]{1,0:T(8,128)(2,1)} %gather_fusion.2) | data formatting | bytes 6291456 | tf_op jit(solution)/shard_map/reshape | solution.py:101
  83.7 106.9 %all_to_all.29 = bf16[64,12,2048]{2,1,0:T(8,128)(2,1)S(1)} all-to-all(bf16[64,12,2048]{2,1,0:T(8,128)(2,1)} %reshape.134), channel_id=1, replica_groups=mesh['ep'=64,'rep'=4] {'ep'}, dimensions={0} | all-to-all | bytes 6291456 | tf_op jit(solution)/shard_map/all_to_all | solution.py:102
  190.6 2.0 copy-done.2
  192.6 0.0 copy-done.12
  192.6 3.1 fusion.9
  195.6 8.8 %convolution_convert_fusion = bf16[64,12,2048]{2,0,1:T(8,128)(2,1)} fusion(bf16[1,352,2048]{2,1,0:T(8,128)(2,1)} %param.33, bf16[1,2048,352]{1,2,0:T(8,128)(2,1)} %param.32, bf16[64,12,2048]{2,1,0:T(8,128)(2,1)} %copy-done.2, f32[64,1,12,352]{3,0,2,1:T(8,128)} %fusion.9), kind=kOutput, calls=%fused_computation.7 | convolution fusion | flops 2217787392 | bytes 10256384 | tf_op jit(solution)/shard_map/secf,efd->secd/dot_general | solution.py:112
  204.4 5.7 %copy.52 = bf16[64,12,2048]{2,1,0:T(8,128)(2,1)} copy(bf16[64,12,2048]{2,0,1:T(8,128)(2,1)} %convolution_convert_fusion) | data formatting | bytes 6291456 | tf_op jit(solution)/shard_map/convert_element_type | solution.py:115
  210.1 5.8 %all-to-all-start.2 = ((bf16[64,12,2048]{2,1,0:T(8,128)(2,1)}), bf16[64,12,2048]{2,1,0:T(8,128)(2,1)}, u32[]{:S(2)}, u32[]{:S(2)}) async-start(bf16[64,12,2048]{2,1,0:T(8,128)(2,1)} %copy.52), calls=%async_computation.2 | async-start | bytes 8388608 | tf_op jit(solution)/shard_map/all_to_all | solution.py:118
  215.9 0.3 reduce-scatter.2.cloned.1.call-start
  216.1 0.0 copy-done.8
  216.1 0.1 copy.53
  216.2 1.9 fusion.80
  218.2 93.9 %all-to-all-done.2 = bf16[64,12,2048]{2,1,0:T(8,128)(2,1)} async-done(((bf16[64,12,2048]{2,1,0:T(8,128)(2,1)}), bf16[64,12,2048]{2,1,0:T(8,128)(2,1)}, u32[]{:S(2)}, u32[]{:S(2)}) %all-to-all-start.2) | async-done | bytes 3145760 | tf_op jit(solution)/shard_map/all_to_all | solution.py:118
  312.0 6.2 %reshape.139 = bf16[768,2048]{1,0:T(8,128)(2,1)} reshape(bf16[64,12,2048]{2,1,0:T(8,128)(2,1)} %all-to-all-done.2) | data formatting | bytes 6291456 | tf_op jit(solution)/shard_map/reshape | solution.py:119
  318.2 7.4 %gather_fusion.3 = bf16[384,2048]{1,0:T(8,128)(2,1)} fusion(bf16[768,2048]{1,0:T(8,128)(2,1)} %reshape.139, s32[1024]{0:T(1024)S(1)} %pad_clamp_fusion), kind=kCustom, calls=%fused_computation.3 | custom fusion | bytes 3147264 | tf_op jit(solution)/shard_map/gather | solution.py:119
  325.6 3.9 %reshape.140 = f32[64,6,2048]{2,1,0:T(8,128)} reshape(bf16[384,2048]{1,0:T(8,128)(2,1)} %gather_fusion.3) | data formatting | bytes 4718592 | tf_op jit(solution)/shard_map/convert_element_type | solution.py:122
  329.5 3.7 %multiply_reduce_fusion = f32[64,2048]{1,0:T(8,128)S(1)} fusion(f32[64,6,2048]{2,1,0:T(8,128)} %reshape.140, f32[64,6]{1,0:T(8,128)S(1)} %copy.53), kind=kLoop, calls=%fused_computation.6 | loop fusion | flops 1441792 | bytes 3671552 | tf_op jit(solution)/shard_map/reduce_sum | solution.py:121
  333.2 0.0 copy-start.7
  333.2 3.7 %fusion.1 = bf16[64,2048]{1,0:T(8,128)(2,1)} fusion(f32[64,2048]{1,0:T(8,128)S(1)} %multiply_reduce_fusion, bf16[352,2048]{1,0:T(8,128)(2,1)} %param.36, bf16[64,2048]{1,0:T(8,128)(2,1)S(1)} %add_convert_fusion, bf16[2048,352]{0,1:T(8,128)(2,1)} %param.35, f32[64,352]{1,0:T(8,128)S(1)} %fusion.80), kind=kOutput, calls=%fused_computation.9 | convolution fusion | flops 184946688 | bytes 4022272 | tf_op jit(solution)/shard_map/dot_general | solution.py:80
  336.9 0.0 reduce-scatter.2.cloned.1.call-update
  337.0 18.5 %reduce-scatter.2.cloned.1.call-done = bf16[16,2048]{1,0:T(8,128)(2,1)} async-done(((bf16[64,2048]{1,0:T(8,128)(2,1)}), bf16[16,2048]{1,0:T(8,128)(2,1)}) %reduce-scatter.2.cloned.1.call-update) | async-done | bytes 65552 | tf_op jit(solution)/shard_map/reduce_scatter | solution.py:127
  355.4 1.0 multiply_reduce_fusion.1
  356.4 1.6 multiply_convert_fusion
  (25 shorter events, 0.2 us)
Async XLA Ops:
  6.5 36.4 %copy-start = (bf16[512,2048]{1,0:T(8,128)(2,1)S(1)}, bf16[512,2048]{1,0:T(8,128)(2,1)}, u32[]{:S(2)}) copy-start(bf16[512,2048]{1,0:T(8,128)(2,1)} %param.27) | copy-start | bytes 6291460
  6.5 65.3 %all-gather.3.cloned.1.call-start = ((), (), s32[]{:S(2)}) async-start(), calls=%async_computation.5 | async-start | bytes 1310720 | tf_op jit(solution)/shard_map/all_gather | solution.py:73
  8.5 8.8 %copy-start.1 = (bf16[32,2048]{1,0:T(8,128)(2,1)S(1)}, bf16[32,2048]{1,0:T(8,128)(2,1)}, u32[]{:S(2)}) copy-start(bf16[32,2048]{1,0:T(8,128)(2,1)} %param.23) | copy-start | bytes 393220
  19.2 3.7 %copy-start.11 = (s32[16]{0:T(128)S(1)}, s32[16]{0:T(128)}, u32[]{:S(2)}) copy-start(s32[16]{0:T(128)} %param.25) | copy-start | bytes 196
  23.0 3.7 %copy-start.6 = (bf16[16,16,64]{2,1,0:T(8,128)(2,1)S(1)}, bf16[16,16,64]{2,1,0:T(8,128)(2,1)}, u32[]{:S(2)}) copy-start(bf16[16,16,64]{2,1,0:T(8,128)(2,1)} %reshape.131) | copy-start | bytes 98308
  27.1 0.8 copy-start.3
  31.7 11.0 %copy-start.4 = (bf16[4,512,128]{2,1,0:T(8,128)(2,1)S(1)}, bf16[4,512,128]{2,1,0:T(8,128)(2,1)}, u32[]{:S(2)}) copy-start(bf16[4,512,128]{2,1,0:T(8,128)(2,1)} %param.26) | copy-start | bytes 1572868
  42.7 1.5 copy-start.9
  42.7 1.5 copy-start.10
  44.1 29.1 %copy-start.5 = (bf16[64,2048]{1,0:T(8,128)(2,1)S(1)}, bf16[64,2048]{1,0:T(8,128)(2,1)}, u32[]{:S(2)}) copy-start(bf16[64,2048]{1,0:T(8,128)(2,1)} %param.19) | copy-start | bytes 786436
  83.7 108.9 %copy-start.12 = (bf16[1,2048,352]{1,2,0:T(8,128)(2,1)S(1)}, bf16[1,2048,352]{1,2,0:T(8,128)(2,1)}, u32[]{:S(2)}) copy-start(bf16[1,2048,352]{1,2,0:T(8,128)(2,1)} %param.31) | copy-start | bytes 4325380
  190.6 2.0 copy-start.2
  210.1 6.0 %copy-start.8 = (f32[64,6]{0,1:T(8,128)S(1)}, f32[64,6]{0,1:T(8,128)}, u32[]{:S(2)}) copy-start(f32[64,6]{0,1:T(8,128)} %param.29) | copy-start | bytes 4612
  210.1 101.9 %all-to-all-start.2 = ((bf16[64,12,2048]{2,1,0:T(8,128)(2,1)}), bf16[64,12,2048]{2,1,0:T(8,128)(2,1)}, u32[]{:S(2)}, u32[]{:S(2)}) async-start(bf16[64,12,2048]{2,1,0:T(8,128)(2,1)} %copy.52), calls=%async_computation.2 | async-start | bytes 8388608 | tf_op jit(solution)/shard_map/all_to_all | solution.py:118
  215.9 139.6 %reduce-scatter.2.cloned.1.call-start = ((), (), s32[]{:S(2)}) async-start(), calls=%async_computation.4 | async-start | bytes 327680 | tf_op jit(solution)/shard_map/reduce_scatter | solution.py:127
  333.2 23.2 %copy-start.7 = (f32[2048]{0:T(1024)S(1)}, f32[2048]{0:T(1024)}, u32[]{:S(2)}) copy-start(f32[2048]{0:T(1024)} %param.37) | copy-start | bytes 24580
Sparse Core Ops, SparseCore 0:
  44.3 27.4 all-gather.2
  337.1 18.3 reduce-scatter.1
